TPU v7x, 32 devices: a whole 2x2x4 slice. The times are simulated.
32 devices in a mesh: groups: 2 (over x), tensor: 16 (over z, y, core).
Axes of the slice: x: 2, y: 2, z: 4, core: 2. Of those that a mesh axis runs over, the one named last changes fastest.
Arguments:
- tokens: bfloat16 [64, 8192], P(('groups', 'tensor')), parts along dimension 0, may hold values from -6 to 6
- cotangent: bfloat16 [64, 8192], P(('groups', 'tensor')), parts along dimension 0, may hold values from -6 to 6
- up_blocks: bfloat16 [512, 128, 128], P('tensor'), may hold values from -0.1875 to 0.1875
- gate_blocks: bfloat16 [512, 128, 128], P('tensor'), may hold values from -0.1875 to 0.1875
- down_blocks: bfloat16 [512, 128, 128], P('tensor'), may hold values from -0.21875 to 0.21875
- up_layout: int32 [512], P('tensor'), may hold values from 0 to 191, as said below
- gate_layout: int32 [512], P('tensor'), may hold values from 0 to 191, as said below
- down_layout: int32 [512], P('tensor'), may hold values from 0 to 191, as said below
- live_counts: int32 [3, 16], P(None, 'tensor'), may hold values from 4 to 32, as said below
Outputs:
- output: bfloat16 [64, 8192], P(('groups', 'tensor')), parts along dimension 0
- grad_tokens: bfloat16 [64, 8192], P(('groups', 'tensor')), parts along dimension 0
- grad_up: bfloat16 [1024, 128, 128], P(('groups', 'tensor')), parts along dimension 0
- grad_gate: bfloat16 [1024, 128, 128], P(('groups', 'tensor')), parts along dimension 0
- grad_down: bfloat16 [1024, 128, 128], P(('groups', 'tensor')), parts along dimension 0
There are 2 independent parts, one for each index of `groups`. A program takes and returns all parts, laid end to end along the dimension named above; an argument that names none is the same for every part. Nothing has to cross between parts.
Inputs may be any that keep to these rules, and one draw needn't show every extreme that they name: `up_layout`: within the 32 slots of one owner the codes of one matrix are all different. `gate_layout`: within the 32 slots of one owner the codes of one matrix are all different. `down_layout`: within the 32 slots of one owner the codes of one matrix are all different. `live_counts`: in each of the three rows some owner has exactly 32 live slots; slots past an owner's count hold blocks that are not used.
All inputs are finite; a program needn't handle non-finite values.
Results may differ from a plain program's by a relative error of at most 0.0051.
Values may be sent and summed in bfloat16 or wider, within the bound.
A program may use at most 64 MiB of HBM per device.

v0:
```python
import jax
import jax.numpy as jnp
from jax import lax
from jax.sharding import PartitionSpec as P

HB_DEV = 3


def slot_tables(layout, count, major_size):
    slot_total = layout.shape[0]
    major = layout // HB_DEV
    minor = layout % HB_DEV
    live_mask = (jnp.arange(slot_total) < count).astype(jnp.float32)
    major_hot = (major[:, None] == jnp.arange(major_size)[None, :]).astype(jnp.float32)
    minor_hot = (minor[:, None] == jnp.arange(HB_DEV)[None, :]).astype(jnp.float32)
    return (major, minor, live_mask, major_hot, minor_hot)


def local(
    tokens,
    cotangent,
    up_blocks,
    gate_blocks,
    down_blocks,
    up_layout,
    gate_layout,
    down_layout,
    live_counts,
):
    highest = lax.Precision.HIGHEST
    f32 = jnp.float32
    x_full = lax.all_gather(tokens, "tensor", axis=0, tiled=True)
    dy_full = lax.all_gather(cotangent, "tensor", axis=0, tiled=True)
    row_total = x_full.shape[0]
    block_size = up_blocks.shape[1]
    width_blocks = x_full.shape[1] // block_size
    x_split = x_full.reshape(row_total, width_blocks, block_size)
    count_trio = live_counts[:, 0]
    up_major, up_minor, up_live, up_rowhot, up_hidhot = slot_tables(
        up_layout, count_trio[0], width_blocks
    )
    gate_major, gate_minor, gate_live, gate_rowhot, gate_hidhot = slot_tables(
        gate_layout, count_trio[1], width_blocks
    )
    down_major, down_minor, down_live, down_colhot, down_hidhot = slot_tables(
        down_layout, count_trio[2], width_blocks
    )
    w_up = up_blocks * up_live[:, None, None].astype(jnp.bfloat16)
    w_gate = gate_blocks * gate_live[:, None, None].astype(jnp.bfloat16)
    w_down = down_blocks * down_live[:, None, None].astype(jnp.bfloat16)
    x_up = jnp.take(x_split, up_major, axis=1)
    x_gate = jnp.take(x_split, gate_major, axis=1)
    up_terms = jnp.einsum("tsi,sij->tsj", x_up, w_up, preferred_element_type=f32)
    gate_terms = jnp.einsum("tsi,sij->tsj", x_gate, w_gate, preferred_element_type=f32)
    up_value = jnp.einsum("tsj,sh->thj", up_terms, up_hidhot, precision=highest)
    gate_value = jnp.einsum("tsj,sh->thj", gate_terms, gate_hidhot, precision=highest)
    sig = 1.0 / (1.0 + jnp.exp(-gate_value))
    act = gate_value * sig
    hidden = (act * up_value).astype(jnp.bfloat16)
    hid_down = jnp.take(hidden, down_minor, axis=1)
    out_terms = jnp.einsum("tsj,sjk->tsk", hid_down, w_down, preferred_element_type=f32)
    partial_out = jnp.einsum("tsk,sc->tck", out_terms, down_colhot, precision=highest).reshape(
        row_total, -1
    )
    out_share = lax.psum_scatter(partial_out, "tensor", scatter_dimension=0, tiled=True)
    dy_split = dy_full.reshape(row_total, width_blocks, block_size)
    dy_down = jnp.take(dy_split, down_major, axis=1)
    dh_terms = jnp.einsum("tsk,sjk->tsj", dy_down, w_down, preferred_element_type=f32)
    d_hidden = jnp.einsum("tsj,sh->thj", dh_terms, down_hidhot, precision=highest)
    d_up = (d_hidden * act).astype(jnp.bfloat16)
    d_gate = (d_hidden * up_value * sig * (1.0 + gate_value * (1.0 - sig))).astype(jnp.bfloat16)
    dup_slots = jnp.take(d_up, up_minor, axis=1)
    dgate_slots = jnp.take(d_gate, gate_minor, axis=1)
    dx_up = jnp.einsum("tsj,sij->tsi", dup_slots, w_up, preferred_element_type=f32)
    dx_gate = jnp.einsum("tsj,sij->tsi", dgate_slots, w_gate, preferred_element_type=f32)
    partial_dx = jnp.einsum("tsi,sr->tri", dx_up, up_rowhot, precision=highest)
    partial_dx = partial_dx + jnp.einsum("tsi,sr->tri", dx_gate, gate_rowhot, precision=highest)
    partial_dx = partial_dx.reshape(row_total, -1)
    dx_share = lax.psum_scatter(partial_dx, "tensor", scatter_dimension=0, tiled=True)
    grad_up = (
        jnp.einsum("tsi,tsj->sij", x_up, dup_slots, preferred_element_type=f32)
        * up_live[:, None, None]
    ).astype(jnp.bfloat16)
    grad_gate = (
        jnp.einsum("tsi,tsj->sij", x_gate, dgate_slots, preferred_element_type=f32)
        * gate_live[:, None, None]
    ).astype(jnp.bfloat16)
    grad_down = (
        jnp.einsum("tsj,tsk->sjk", hid_down, dy_down, preferred_element_type=f32)
        * down_live[:, None, None]
    ).astype(jnp.bfloat16)
    return (
        out_share.astype(jnp.bfloat16),
        dx_share.astype(jnp.bfloat16),
        grad_up,
        grad_gate,
        grad_down,
    )


def solution(mesh):
    placed = (
        P(("groups", "tensor"), None),
        P(("groups", "tensor"), None),
        P("tensor", None, None),
        P("tensor", None, None),
        P("tensor", None, None),
        P("tensor"),
        P("tensor"),
        P("tensor"),
        P(None, "tensor"),
    )
    return jax.shard_map(
        local,
        mesh=mesh,
        in_specs=placed,
        out_specs=(
            P(("groups", "tensor"), None),
            P(("groups", "tensor"), None),
            P(("groups", "tensor"), None, None),
            P(("groups", "tensor"), None, None),
            P(("groups", "tensor"), None, None),
        ),
        check_vma=False,
    )
```

profile of v0, /device:TPU:0, one launch (start us, length us, event | category | flops | bytes accessed | tf_op | source)
XLA Modules:
  0.0 150.8 jit_solution(14236068998945516922)
XLA Ops:
  0.6 0.7 compare_and_fusion.1
  1.3 24.8 %all-gather = bf16[16,2,8192]{2,1,0:T(2,128)(2,1)S(1)} all-gather(bf16[1,2,8192]{2,1,0:T(2,128)(2,1)} %bitcast.118), channel_id=1, replica_groups=mesh['groups'=2,'tensor'=16] {'tensor'}, dimensions={0}, use_global_device_ids=true | all-gather | bytes 557056 | tf_op jit(solution)/shard_map/all_gather | solution.py:32
  26.1 0.4 reshape.71
  26.5 0.0 copy-start.4
  26.5 0.0 copy-start
  26.5 0.3 copy.44
  26.9 0.6 gather_fusion.1
  27.5 0.6 fusion.74
  28.1 0.6 fusion.73
  28.8 0.0 copy-done
  28.8 0.0 copy-start.5
  28.8 0.5 convolution_bitcast_fusion.1
  29.3 0.6 fusion.13
  29.9 0.6 gather_fusion
  30.5 0.6 fusion.72
  31.2 0.0 copy-start.6
  31.2 0.0 copy-start.3
  31.2 1.7 %convolution_bitcast_fusion.2 = f32[32,32,128]{2,0,1:T(8,128)S(1)} fusion(bf16[32,128,128]{2,1,0:T(8,128)(2,1)} %param.16, bf16[32]{0:T(256)(128)(2,1)S(1)} %fusion.72, bf16[32,32,128]{2,1,0:T(8,128)(2,1)S(1)} %gather_fusion, pred[32]{0:T(512)(128)(4,1)S(1)} %get-tuple-element.26), kind=kOutput, calls=%fused_computation.12 | convolution fusion | flops 35782656 | bytes 1835104 | tf_op jit(solution)/shard_map/tsi,sij->tsj/dot_general | solution.py:54
  32.9 0.6 fusion.15
  33.5 18.9 %all-gather.1 = bf16[16,2,8192]{2,1,0:T(2,128)(2,1)S(1)} all-gather(bf16[1,2,8192]{2,1,0:T(2,128)(2,1)S(1)} %bitcast.119), channel_id=1, replica_groups=mesh['groups'=2,'tensor'=16] {'tensor'}, dimensions={0}, use_global_device_ids=true | all-gather | bytes 557056 | tf_op jit(solution)/shard_map/all_gather | solution.py:33
  52.4 0.4 reshape.73
  52.8 0.3 copy.51
  53.2 0.6 gather_fusion.3
  53.8 0.6 fusion.71
  54.3 1.9 %convolution_bitcast_fusion.5 = f32[32,32,128]{2,0,1:T(8,128)S(1)} fusion(bf16[32,128,128]{2,1,0:T(8,128)(2,1)} %param.17, bf16[32]{0:T(256)(128)(2,1)S(1)} %fusion.71, bf16[32,32,128]{2,1,0:T(8,128)(2,1)S(1)} %gather_fusion.3, pred[32]{0:T(512)(128)(4,1)S(1)} %get-tuple-element.13), kind=kOutput, calls=%fused_computation.15 | convolution fusion | flops 34209792 | bytes 1835104 | tf_op jit(solution)/shard_map/tsk,sjk->tsj/dot_general | solution.py:68
  56.3 0.6 fusion.9
  57.0 0.6 gather_fusion.4
  57.6 0.7 convolution_bitcast_fusion.4
  58.3 0.9 fusion.7
  59.3 1.3 gather_fusion.5
  60.6 1.7 %convolution_bitcast_fusion.3 = f32[32,32,128]{2,0,1:T(8,128)S(1)} fusion(bf16[32,128,128]{2,1,0:T(8,128)(2,1)S(1)} %copy-done.1, bf16[32]{0:T(256)(128)(2,1)S(1)} %fusion.72, bf16[32,32,128]{2,1,0:T(8,128)(2,1)} %gather_fusion.5, pred[32]{0:T(512)(128)(4,1)S(1)} %get-tuple-element.9), kind=kOutput, calls=%fused_computation.13 | convolution fusion | flops 34209792 | bytes 1835104 | tf_op jit(solution)/shard_map/tsj,sij->tsi/dot_general | solution.py:75
  62.2 1.0 convolution_add_fusion
  63.2 0.0 copy-start.2
  63.2 0.6 copy.82
  63.9 0.6 gather_fusion.2
  64.5 0.5 convolution_bitcast_fusion
  65.0 0.9 fusion.11
  65.9 0.6 copy.83
  66.5 0.0 copy-start.7
  66.5 73.7 %all-reduce.4 = (bf16[32,8192]{1,0:T(8,128)(2,1)}, bf16[32,8192]{1,0:T(8,128)(2,1)}) all-reduce(f32[32,8192]{1,0:T(8,128)S(1)} %bitcast.115, f32[32,8192]{1,0:T(8,128)S(1)} %bitcast.114), channel_id=2, replica_groups=mesh['groups'=2,'tensor'=16] {'tensor'}, use_global_device_ids=true, to_apply=%region_0.3.clone | all-reduce | flops 524288 | bytes 3145728
  140.2 0.6 dynamic-slice
  141.4 1.7 %dynamic-slice_convert_fusion = (bf16[2,8192]{1,0:T(2,128)(2,1)}, bf16[2,8192]{1,0:T(2,128)(2,1)}) fusion(bf16[32,8192]{1,0:T(8,128)(2,1)} %get-tuple-element.8, u32[]{:T(128)S(6)} %multiply.1, bf16[32,8192]{1,0:T(8,128)(2,1)} %get-tuple-element.7), kind=kLoop, calls=%fused_computation.59 | loop fusion | bytes 131076 | tf_op jit(solution)/shard_map/convert_element_type | solution.py:94
  143.1 0.6 compare_convert_fusion.1
  143.8 2.6 %multiply_convert_fusion.1 = bf16[32,128,128]{2,1,0:T(8,128)(2,1)} fusion(f32[32]{0:T(128)S(1)} %compare_convert_fusion.1, bf16[32,32,128]{2,1,0:T(8,128)(2,1)S(1)} %gather_fusion, pred[32]{0:T(512)(128)(4,1)S(1)} %get-tuple-element.26, bf16[32,32,128]{2,1,0:T(8,128)(2,1)} %gather_fusion.5, pred[32]{0:T(512)(128)(4,1)S(1)} %get-tuple-element.9), kind=kOutput, calls=%fused_computation.7 | convolution fusion | flops 34865152 | bytes 1573056 | tf_op jit(solution)/shard_map/tsi,tsj->sij/dot_general | solution.py:85
  146.3 0.6 compare_convert_fusion
  147.0 1.6 %multiply_convert_fusion.2 = bf16[32,128,128]{2,1,0:T(8,128)(2,1)} fusion(f32[32]{0:T(128)S(1)} %compare_convert_fusion, bf16[32,32,128]{2,1,0:T(8,128)(2,1)S(1)} %gather_fusion.1, pred[32]{0:T(512)(128)(4,1)S(1)} %get-tuple-element.31, bf16[32,32,128]{2,1,0:T(8,128)(2,1)S(1)} %gather_fusion.4, pred[32]{0:T(512)(128)(4,1)S(1)} %get-tuple-element.11), kind=kOutput, calls=%fused_computation.8 | convolution fusion | flops 34865152 | bytes 1573056 | tf_op jit(solution)/shard_map/tsi,tsj->sij/dot_general | solution.py:81
  148.6 0.6 compare_convert_fusion.2
  149.2 1.6 %multiply_convert_fusion = bf16[32,128,128]{2,1,0:T(8,128)(2,1)} fusion(f32[32]{0:T(128)S(1)} %compare_convert_fusion.2, bf16[32,32,128]{2,1,0:T(8,128)(2,1)S(1)} %gather_fusion.2, pred[32]{0:T(512)(128)(4,1)S(1)} %get-tuple-element.24, bf16[32,32,128]{2,1,0:T(8,128)(2,1)S(1)} %gather_fusion.3, pred[32]{0:T(512)(128)(4,1)S(1)} %get-tuple-element.13), kind=kOutput, calls=%fused_computation.6 | convolution fusion | flops 34865152 | bytes 1573056 | tf_op jit(solution)/shard_map/tsj,tsk->sjk/dot_general | solution.py:89
  (23 shorter events, 0.2 us)
Async XLA Ops:
  26.5 1.0 copy-start.4
  26.5 2.2 %copy-start = (bf16[32,128,128]{2,1,0:T(8,128)(2,1)S(1)}, bf16[32,128,128]{2,1,0:T(8,128)(2,1)}, u32[]{:S(2)}) copy-start(bf16[32,128,128]{2,1,0:T(8,128)(2,1)} %param.15) | copy-start | bytes 3145732
  28.8 1.1 copy-start.5
  31.2 2.3 %copy-start.6 = (s32[32]{0:T(128)S(1)}, s32[32]{0:T(128)}, u32[]{:S(2)}) copy-start(s32[32]{0:T(128)} %param.20) | copy-start | bytes 388
  31.2 2.4 %copy-start.3 = (bf16[2,8192]{1,0:T(2,128)(2,1)S(1)}, bf16[2,8192]{1,0:T(2,128)(2,1)}, u32[]{:S(2)}) copy-start(bf16[2,8192]{1,0:T(2,128)(2,1)} %param.14) | copy-start | bytes 98308
  58.3 2.3 %copy-start.1 = (bf16[32,128,128]{2,1,0:T(8,128)(2,1)S(1)}, bf16[32,128,128]{2,1,0:T(8,128)(2,1)}, u32[]{:S(2)}) copy-start(bf16[32,128,128]{2,1,0:T(8,128)(2,1)} %param.16) | copy-start | bytes 3145732
  63.2 1.3 copy-start.2
  66.5 73.7 %copy-start.7 = (u32[32]{0:T(128)S(1)}, u32[32]{0:T(128)}, u32[]{:S(2)}) copy-start(u32[32]{0:T(128)} %constant.59) | copy-start | bytes 388
where the time goes:
time: 151 us
  blocking collectives  117 us (77%)
  matrix products  17.4 us (12%)
  local copies, waits for them, and re-layouts  9.91 us (7%)
  other arithmetic  4.48 us (3%)
  between operations  1.65 us (1%)
    unnamed x1, blocking collectives  73.7 us
    all_gather x1, blocking collectives, local(): x_full = lax.all_gather(tokens, 'tensor', axis=0, tiled=True)  24.8 us
    all_gather x1, blocking collectives, local(): dy_full = lax.all_gather(cotangent, 'tensor', axis=0, tiled=True)  18.9 us

commit v1 on v0

--- a/solution.py
+++ b/solution.py
@@ -4,6 +4,28 @@
 from jax.sharding import PartitionSpec as P
 
 HB_DEV = 3
+
+
+def joined_along(pieces, dim):
+    shape = list(pieces.shape[1:])
+    shape[dim] *= pieces.shape[0]
+    return jnp.moveaxis(pieces, 0, dim).reshape(shape)
+
+
+def collect(value, axis, dim):
+    size = lax.axis_size(axis)
+    pairs = [(i, (i + 1) % size) for i in range(size)]
+    back = [(b, a) for a, b in pairs]
+    lower, upper = ([], [])
+    for step in range(size - 1):
+        if step % 2 == 0:
+            lower.append(lax.ppermute(lower[-1] if lower else value, axis, pairs))
+        else:
+            upper.append(lax.ppermute(upper[-1] if upper else value, axis, back))
+    blocks = jnp.stack([*lower[::-1], value, *upper])
+    shift = lax.axis_index(axis) - len(lower)
+    blocks = blocks[(jnp.arange(size) - shift) % size]
+    return joined_along(blocks, dim)
 
 
 def slot_tables(layout, count, major_size):
@@ -29,7 +51,7 @@
 ):
     highest = lax.Precision.HIGHEST
     f32 = jnp.float32
-    x_full = lax.all_gather(tokens, "tensor", axis=0, tiled=True)
+    x_full = collect(tokens, "tensor", 0)
     dy_full = lax.all_gather(cotangent, "tensor", axis=0, tiled=True)
     row_total = x_full.shape[0]
     block_size = up_blocks.shape[1]

time: 151 us -> 181 us (1.20)
  starting transfers between devices: 0 us -> 32.9 us
  blocking collectives: 117 us -> 97.7 us
  waiting for transfers between devices: 0 us -> 10.5 us
  local copies, waits for them, and re-layouts: 9.91 us -> 14.6 us
  other arithmetic: 4.48 us -> 7.86 us
  matrix products: 17.4 us -> 14.9 us
    ppermute x0 -> x15, starting transfers between devices: none -> 32.9 us  [the longest x7 32 us: collect(): upper.append(lax.ppermute(upper[-1] if upper else value, axis, back))]
    all_gather x1 -> x0, blocking collectives: 24.8 us -> none  [local(): x_full = lax.all_gather(tokens, 'tensor', axis=0, tiled=True)]
    ppermute x0 -> x15, waiting for transfers between devices: none -> 10.5 us  [the longest x8 9.28 us: collect(): lower.append(lax.ppermute(lower[-1] if lower else value, axis, pairs))]
    unnamed x1, blocking collectives: 73.7 us -> 76.6 us
    all_gather x1, blocking collectives: 18.9 us -> 21 us  [local(): dy_full = lax.all_gather(cotangent, 'tensor', axis=0, tiled=True)]
  transfers between devices with their start and end apart: 0 -> 15, of which waited for: 0 -> 9; matrix products, arithmetic and copies ran while one was open for 0% -> 7% of each run, Pallas kernels for 0% -> 0%
where the time goes in v1:
time: 181 us; the launch traced here: 180 us
  blocking collectives  97.7 us (54%)
  starting transfers between devices  32.9 us (18%)
  matrix products  14.9 us (8%)
  local copies, waits for them, and re-layouts  14.6 us (8%)
  waiting for transfers between devices  10.5 us (6%)
  other arithmetic  7.86 us (4%)
  between operations  1.94 us (1%)
    unnamed x1, blocking collectives  76.6 us
    ppermute x7, starting transfers between devices, collect(): upper.append(lax.ppermute(upper[-1] if upper else value, axis, back))  32 us
    all_gather x1, blocking collectives, local(): dy_full = lax.all_gather(cotangent, 'tensor', axis=0, tiled=True)  21 us
    ppermute x8, waiting for transfers between devices, collect(): lower.append(lax.ppermute(lower[-1] if lower else value, axis, pairs))  9.28 us
  transfers between devices with their start and end apart: 15, of which 9 were waited for; matrix products, arithmetic and copies ran while one was open for 7% of the time, Pallas kernels for 0%

profile of v1, /device:TPU:0, one launch (start us, length us, event | category | flops | bytes accessed | tf_op | source)
XLA Modules:
  0.0 180.3 jit_solution(3931051904053956462)
XLA Ops:
  1.1 5.1 %collective-permute-start.8 = (bf16[2,8192]{1,0:T(2,128)(2,1)}, bf16[2,8192]{1,0:T(2,128)(2,1)S(1)}, u32[]{:S(2)}, u32[]{:S(2)}) collective-permute-start(bf16[2,8192]{1,0:T(2,128)(2,1)} %param.13), channel_id=1, source_target_pairs={{1,0},{2,1},{3,2},{4,3},{5,4},{6,5},{7,6},{8,7},{9,8},{10,9},{11,1... | collective-permute-start | bytes 98312 | tf_op jit(solution)/shard_map/ppermute | solution.py:24
  6.2 1.4 fusion.76
  7.6 0.6 fusion.73
  8.2 21.0 %all-gather = bf16[16,2,8192]{2,1,0:T(2,128)(2,1)S(1)} all-gather(bf16[1,2,8192]{2,1,0:T(2,128)(2,1)} %bitcast.151), channel_id=1, replica_groups=mesh['groups'=2,'tensor'=16] {'tensor'}, dimensions={0}, use_global_device_ids=true | all-gather | bytes 557056 | tf_op jit(solution)/shard_map/all_gather | solution.py:55
  30.6 0.6 copy-done.11
  31.1 0.6 gather_fusion.4
  31.8 0.7 convolution_bitcast_fusion.5
  32.5 0.6 fusion.9
  33.1 0.6 compare_and_fusion.1
  33.8 0.6 compare_and_fusion
  34.9 5.7 %collective-permute-done.1 = bf16[2,8192]{1,0:T(2,128)(2,1)S(1)} collective-permute-done((bf16[2,8192]{1,0:T(2,128)(2,1)S(1)}, bf16[2,8192]{1,0:T(2,128)(2,1)S(1)}, u32[]{:S(2)}, u32[]{:S(2)}) %collective-permute-start.1) | collective-permute-done | bytes 32800 | tf_op jit(solution)/shard_map/ppermute | solution.py:22
  40.6 4.5 %collective-permute-start.9 = (bf16[2,8192]{1,0:T(2,128)(2,1)S(1)}, bf16[2,8192]{1,0:T(2,128)(2,1)S(1)}, u32[]{:S(2)}, u32[]{:S(2)}) collective-permute-start(bf16[2,8192]{1,0:T(2,128)(2,1)S(1)} %collective-permute-done.8), channel_id=1, source_target_pairs={{1,0},{2,1},{3,2},{4,3},{5,4},{6,5},{7,6},{8,7},{9,8},{10,9},{11,1... | collective-permute-start | bytes 98312 | tf_op jit(solution)/shard_map/ppermute | solution.py:24
  45.0 1.5 collective-permute-done.2
  46.6 0.6 fusion.75
  47.3 4.5 %collective-permute-start.10 = (bf16[2,8192]{1,0:T(2,128)(2,1)S(1)}, bf16[2,8192]{1,0:T(2,128)(2,1)S(1)}, u32[]{:S(2)}, u32[]{:S(2)}) collective-permute-start(bf16[2,8192]{1,0:T(2,128)(2,1)S(1)} %collective-permute-done.9), channel_id=1, source_target_pairs={{1,0},{2,1},{3,2},{4,3},{5,4},{6,5},{7,6},{8,7},{9,8},{10,9},{11,1... | collective-permute-start | bytes 98312 | tf_op jit(solution)/shard_map/ppermute | solution.py:24
  51.8 1.0 collective-permute-done.3
  52.7 1.2 compare_convert_fusion
  54.0 4.4 %collective-permute-start.11 = (bf16[2,8192]{1,0:T(2,128)(2,1)S(1)}, bf16[2,8192]{1,0:T(2,128)(2,1)S(1)}, u32[]{:S(2)}, u32[]{:S(2)}) collective-permute-start(bf16[2,8192]{1,0:T(2,128)(2,1)S(1)} %collective-permute-done.10), channel_id=1, source_target_pairs={{1,0},{2,1},{3,2},{4,3},{5,4},{6,5},{7,6},{8,7},{9,8},{10,9},{11,1... | collective-permute-start | bytes 98312 | tf_op jit(solution)/shard_map/ppermute | solution.py:24
  58.8 1.2 fusion.74
  60.0 4.4 %collective-permute-start.12 = (bf16[2,8192]{1,0:T(2,128)(2,1)S(1)}, bf16[2,8192]{1,0:T(2,128)(2,1)S(1)}, u32[]{:S(2)}, u32[]{:S(2)}) collective-permute-start(bf16[2,8192]{1,0:T(2,128)(2,1)S(1)} %collective-permute-done.11), channel_id=1, source_target_pairs={{1,0},{2,1},{3,2},{4,3},{5,4},{6,5},{7,6},{8,7},{9,8},{10,9},{11,1... | collective-permute-start | bytes 98312 | tf_op jit(solution)/shard_map/ppermute | solution.py:24
  64.8 1.2 compare_convert_fusion.1
  66.0 4.4 %collective-permute-start.13 = (bf16[2,8192]{1,0:T(2,128)(2,1)S(1)}, bf16[2,8192]{1,0:T(2,128)(2,1)S(1)}, u32[]{:S(2)}, u32[]{:S(2)}) collective-permute-start(bf16[2,8192]{1,0:T(2,128)(2,1)S(1)} %collective-permute-done.12), channel_id=1, source_target_pairs={{1,0},{2,1},{3,2},{4,3},{5,4},{6,5},{7,6},{8,7},{9,8},{10,9},{11,1... | collective-permute-start | bytes 98312 | tf_op jit(solution)/shard_map/ppermute | solution.py:24
  70.8 1.2 compare_convert_fusion.2
  72.0 0.6 dynamic-slice
  73.3 4.7 %collective-permute-start.14 = (bf16[2,8192]{1,0:T(2,128)(2,1)S(1)}, bf16[2,8192]{1,0:T(2,128)(2,1)S(1)}, u32[]{:S(2)}, u32[]{:S(2)}) collective-permute-start(bf16[2,8192]{1,0:T(2,128)(2,1)S(1)} %collective-permute-done.13), channel_id=1, source_target_pairs={{1,0},{2,1},{3,2},{4,3},{5,4},{6,5},{7,6},{8,7},{9,8},{10,9},{11,1... | collective-permute-start | bytes 98312 | tf_op jit(solution)/shard_map/ppermute | solution.py:24
  78.5 1.0 collective-permute-done.14
  79.6 1.6 gather_fusion
  82.0 0.6 gather_fusion.2
  83.3 0.6 fusion.13
  83.9 0.6 gather_fusion.1
  84.5 1.1 convolution_bitcast_fusion.2
  85.7 0.6 fusion.15
  86.3 0.6 gather_fusion.3
  87.6 0.9 fusion.11
  88.5 0.6 copy.83
  89.2 0.6 gather_fusion.5
  89.8 0.7 convolution_bitcast_fusion.4
  90.5 0.9 fusion.7
  91.5 0.6 gather_fusion.6
  92.1 1.9 %convolution_bitcast_fusion.3 = f32[32,32,128]{2,0,1:T(8,128)S(1)} fusion(bf16[32,128,128]{2,1,0:T(8,128)(2,1)} %param.16, bf16[32]{0:T(256)(128)(2,1)S(1)} %copy-done.25, bf16[32,32,128]{2,1,0:T(8,128)(2,1)S(1)} %gather_fusion.6, pred[32]{0:T(512)(128)(4,1)S(1)} %copy-done.32), kind=kOutput, calls=%fused_computation.14 | convolution fusion | flops 34209792 | bytes 1835104 | tf_op jit(solution)/shard_map/tsj,sij->tsi/dot_general | solution.py:97
  94.1 0.9 convolution_add_fusion
  95.0 0.6 copy.82
  95.7 76.6 %all-reduce.4 = (bf16[32,8192]{1,0:T(8,128)(2,1)}, bf16[32,8192]{1,0:T(8,128)(2,1)}) all-reduce(f32[32,8192]{1,0:T(8,128)S(1)} %bitcast.147, f32[32,8192]{1,0:T(8,128)S(1)} %bitcast.148), channel_id=2, replica_groups=mesh['groups'=2,'tensor'=16] {'tensor'}, use_global_device_ids=true, to_apply=%region_0.3.clone | all-reduce | flops 524288 | bytes 3145728
  172.3 1.6 dynamic-slice_convert_fusion.1
  173.9 1.6 dynamic-slice_convert_fusion
  175.4 1.6 multiply_convert_fusion.2
  177.1 1.6 multiply_convert_fusion.1
  178.7 1.6 multiply_convert_fusion
  (127 shorter events, 6.3 us)
Async XLA Ops:
  0.6 33.8 %collective-permute-start = (bf16[2,8192]{1,0:T(2,128)(2,1)}, bf16[2,8192]{1,0:T(2,128)(2,1)S(1)}, u32[]{:S(2)}, u32[]{:S(2)}) collective-permute-start(bf16[2,8192]{1,0:T(2,128)(2,1)} %param.13), channel_id=1, source_target_pairs={{0,1},{1,2},{2,3},{3,4},{4,5},{5,6},{6,7},{7,8},{8,9},{9,10},{10,1... | collective-permute-start | bytes 98312 | tf_op jit(solution)/shard_map/ppermute | solution.py:22
  1.1 39.4 %collective-permute-start.8 = (bf16[2,8192]{1,0:T(2,128)(2,1)}, bf16[2,8192]{1,0:T(2,128)(2,1)S(1)}, u32[]{:S(2)}, u32[]{:S(2)}) collective-permute-start(bf16[2,8192]{1,0:T(2,128)(2,1)} %param.13), channel_id=1, source_target_pairs={{1,0},{2,1},{3,2},{4,3},{5,4},{6,5},{7,6},{8,7},{9,8},{10,9},{11,1... | collective-permute-start | bytes 98312 | tf_op jit(solution)/shard_map/ppermute | solution.py:24
  8.2 23.5 %copy-start.21 = (bf16[32]{0:T(256)(128)(2,1)}, bf16[32]{0:T(256)(128)(2,1)S(1)}, u32[]{:S(2)}) copy-start(bf16[32]{0:T(256)(128)(2,1)S(1)} %fusion.73) | copy-start | bytes 196
  29.2 0.8 copy-start.26
  29.6 2.1 %copy-start = (bf16[32,128,128]{2,1,0:T(8,128)(2,1)S(1)}, bf16[32,128,128]{2,1,0:T(8,128)(2,1)}, u32[]{:S(2)}) copy-start(bf16[32,128,128]{2,1,0:T(8,128)(2,1)} %param.17) | copy-start | bytes 3145732
  30.5 2.0 %copy-start.29 = (pred[32]{0:T(512)(128)(4,1)}, pred[32]{0:T(512)(128)(4,1)S(1)}, u32[]{:S(2)}) copy-start(pred[32]{0:T(512)(128)(4,1)S(1)} %get-tuple-element.13) | copy-start | bytes 100
  31.7 1.4 copy-start.4
  31.8 1.4 copy-start.27
  31.8 2.0 %copy-start.28 = (s32[32]{0:T(128)S(1)}, s32[32]{0:T(128)}, u32[]{:S(2)}) copy-start(s32[32]{0:T(128)} %param.19) | copy-start | bytes 388
  31.8 40.2 %copy-start.33 = (u32[32]{0:T(128)S(1)}, u32[32]{0:T(128)}, u32[]{:S(2)}) copy-start(u32[32]{0:T(128)} %constant.82) | copy-start | bytes 388
  32.5 45.7 %copy-start.6 = (bf16[2,8192]{1,0:T(2,128)(2,1)S(1)}, bf16[2,8192]{1,0:T(2,128)(2,1)}, u32[]{:S(2)}) copy-start(bf16[2,8192]{1,0:T(2,128)(2,1)} %param.13) | copy-start | bytes 98308
  33.7 47.4 %copy-start.17 = (s32[32]{0:T(128)}, s32[32]{0:T(128)S(1)}, u32[]{:S(2)}) copy-start(s32[32]{0:T(128)S(1)} %get-tuple-element.12) | copy-start | bytes 388
  33.8 48.8 %copy-start.8 = (pred[32]{0:T(512)(128)(4,1)}, pred[32]{0:T(512)(128)(4,1)S(1)}, u32[]{:S(2)}) copy-start(pred[32]{0:T(512)(128)(4,1)S(1)} %get-tuple-element.31) | copy-start | bytes 100
  34.4 46.8 %copy-start.15 = (s32[32]{0:T(128)}, s32[32]{0:T(128)S(1)}, u32[]{:S(2)}) copy-start(s32[32]{0:T(128)S(1)} %get-tuple-element.10) | copy-start | bytes 388
  34.4 46.8 %copy-start.19 = (s32[32]{0:T(128)}, s32[32]{0:T(128)S(1)}, u32[]{:S(2)}) copy-start(s32[32]{0:T(128)S(1)} %get-tuple-element.27) | copy-start | bytes 388
  34.5 6.1 %collective-permute-start.1 = (bf16[2,8192]{1,0:T(2,128)(2,1)S(1)}, bf16[2,8192]{1,0:T(2,128)(2,1)S(1)}, u32[]{:S(2)}, u32[]{:S(2)}) collective-permute-start(bf16[2,8192]{1,0:T(2,128)(2,1)S(1)} %collective-permute-done), channel_id=1, source_target_pairs={{0,1},{1,2},{2,3},{3,4},{4,5},{5,6},{6,7},{7,8},{8,9},{9,10},{10,1... | collective-permute-start | bytes 98312 | tf_op jit(solution)/shard_map/ppermute | solution.py:22
  40.5 6.0 %collective-permute-start.2 = (bf16[2,8192]{1,0:T(2,128)(2,1)S(1)}, bf16[2,8192]{1,0:T(2,128)(2,1)S(1)}, u32[]{:S(2)}, u32[]{:S(2)}) collective-permute-start(bf16[2,8192]{1,0:T(2,128)(2,1)S(1)} %collective-permute-done.1), channel_id=1, source_target_pairs={{0,1},{1,2},{2,3},{3,4},{4,5},{5,6},{6,7},{7,8},{8,9},{9,10},{10,1... | collective-permute-start | bytes 98312 | tf_op jit(solution)/shard_map/ppermute | solution.py:22
  40.6 6.7 %collective-permute-start.9 = (bf16[2,8192]{1,0:T(2,128)(2,1)S(1)}, bf16[2,8192]{1,0:T(2,128)(2,1)S(1)}, u32[]{:S(2)}, u32[]{:S(2)}) collective-permute-start(bf16[2,8192]{1,0:T(2,128)(2,1)S(1)} %collective-permute-done.8), channel_id=1, source_target_pairs={{1,0},{2,1},{3,2},{4,3},{5,4},{6,5},{7,6},{8,7},{9,8},{10,9},{11,1... | collective-permute-start | bytes 98312 | tf_op jit(solution)/shard_map/ppermute | solution.py:24
  46.6 6.1 %collective-permute-start.3 = (bf16[2,8192]{1,0:T(2,128)(2,1)S(1)}, bf16[2,8192]{1,0:T(2,128)(2,1)S(1)}, u32[]{:S(2)}, u32[]{:S(2)}) collective-permute-start(bf16[2,8192]{1,0:T(2,128)(2,1)S(1)} %collective-permute-done.2), channel_id=1, source_target_pairs={{0,1},{1,2},{2,3},{3,4},{4,5},{5,6},{6,7},{7,8},{8,9},{9,10},{10,1... | collective-permute-start | bytes 98312 | tf_op jit(solution)/shard_map/ppermute | solution.py:22
  47.2 35.4 %copy-start.23 = (bf16[32]{0:T(256)(128)(2,1)}, bf16[32]{0:T(256)(128)(2,1)S(1)}, u32[]{:S(2)}) copy-start(bf16[32]{0:T(256)(128)(2,1)S(1)} %fusion.75) | copy-start | bytes 196
  47.3 6.7 %collective-permute-start.10 = (bf16[2,8192]{1,0:T(2,128)(2,1)S(1)}, bf16[2,8192]{1,0:T(2,128)(2,1)S(1)}, u32[]{:S(2)}, u32[]{:S(2)}) collective-permute-start(bf16[2,8192]{1,0:T(2,128)(2,1)S(1)} %collective-permute-done.9), channel_id=1, source_target_pairs={{1,0},{2,1},{3,2},{4,3},{5,4},{6,5},{7,6},{8,7},{9,8},{10,9},{11,1... | collective-permute-start | bytes 98312 | tf_op jit(solution)/shard_map/ppermute | solution.py:24
  52.7 6.0 %collective-permute-start.4 = (bf16[2,8192]{1,0:T(2,128)(2,1)S(1)}, bf16[2,8192]{1,0:T(2,128)(2,1)S(1)}, u32[]{:S(2)}, u32[]{:S(2)}) collective-permute-start(bf16[2,8192]{1,0:T(2,128)(2,1)S(1)} %collective-permute-done.3), channel_id=1, source_target_pairs={{0,1},{1,2},{2,3},{3,4},{4,5},{5,6},{6,7},{7,8},{8,9},{9,10},{10,1... | collective-permute-start | bytes 98312 | tf_op jit(solution)/shard_map/ppermute | solution.py:22
  54.0 6.0 %collective-permute-start.11 = (bf16[2,8192]{1,0:T(2,128)(2,1)S(1)}, bf16[2,8192]{1,0:T(2,128)(2,1)S(1)}, u32[]{:S(2)}, u32[]{:S(2)}) collective-permute-start(bf16[2,8192]{1,0:T(2,128)(2,1)S(1)} %collective-permute-done.10), channel_id=1, source_target_pairs={{1,0},{2,1},{3,2},{4,3},{5,4},{6,5},{7,6},{8,7},{9,8},{10,9},{11,1... | collective-permute-start | bytes 98312 | tf_op jit(solution)/shard_map/ppermute | solution.py:24
  58.8 6.0 %collective-permute-start.5 = (bf16[2,8192]{1,0:T(2,128)(2,1)S(1)}, bf16[2,8192]{1,0:T(2,128)(2,1)S(1)}, u32[]{:S(2)}, u32[]{:S(2)}) collective-permute-start(bf16[2,8192]{1,0:T(2,128)(2,1)S(1)} %collective-permute-done.4), channel_id=1, source_target_pairs={{0,1},{1,2},{2,3},{3,4},{4,5},{5,6},{6,7},{7,8},{8,9},{9,10},{10,1... | collective-permute-start | bytes 98312 | tf_op jit(solution)/shard_map/ppermute | solution.py:22
  60.0 6.0 %collective-permute-start.12 = (bf16[2,8192]{1,0:T(2,128)(2,1)S(1)}, bf16[2,8192]{1,0:T(2,128)(2,1)S(1)}, u32[]{:S(2)}, u32[]{:S(2)}) collective-permute-start(bf16[2,8192]{1,0:T(2,128)(2,1)S(1)} %collective-permute-done.11), channel_id=1, source_target_pairs={{1,0},{2,1},{3,2},{4,3},{5,4},{6,5},{7,6},{8,7},{9,8},{10,9},{11,1... | collective-permute-start | bytes 98312 | tf_op jit(solution)/shard_map/ppermute | solution.py:24
  64.8 6.0 %collective-permute-start.6 = (bf16[2,8192]{1,0:T(2,128)(2,1)S(1)}, bf16[2,8192]{1,0:T(2,128)(2,1)S(1)}, u32[]{:S(2)}, u32[]{:S(2)}) collective-permute-start(bf16[2,8192]{1,0:T(2,128)(2,1)S(1)} %collective-permute-done.5), channel_id=1, source_target_pairs={{0,1},{1,2},{2,3},{3,4},{4,5},{5,6},{6,7},{7,8},{8,9},{9,10},{10,1... | collective-permute-start | bytes 98312 | tf_op jit(solution)/shard_map/ppermute | solution.py:22
  66.0 7.2 %collective-permute-start.13 = (bf16[2,8192]{1,0:T(2,128)(2,1)S(1)}, bf16[2,8192]{1,0:T(2,128)(2,1)S(1)}, u32[]{:S(2)}, u32[]{:S(2)}) collective-permute-start(bf16[2,8192]{1,0:T(2,128)(2,1)S(1)} %collective-permute-done.12), channel_id=1, source_target_pairs={{1,0},{2,1},{3,2},{4,3},{5,4},{6,5},{7,6},{8,7},{9,8},{10,9},{11,1... | collective-permute-start | bytes 98312 | tf_op jit(solution)/shard_map/ppermute | solution.py:24
  70.8 7.1 %collective-permute-start.7 = (bf16[2,8192]{1,0:T(2,128)(2,1)S(1)}, bf16[2,8192]{1,0:T(2,128)(2,1)S(1)}, u32[]{:S(2)}, u32[]{:S(2)}) collective-permute-start(bf16[2,8192]{1,0:T(2,128)(2,1)S(1)} %collective-permute-done.6), channel_id=1, source_target_pairs={{0,1},{1,2},{2,3},{3,4},{4,5},{5,6},{6,7},{7,8},{8,9},{9,10},{10,1... | collective-permute-start | bytes 98312 | tf_op jit(solution)/shard_map/ppermute | solution.py:22
  73.3 6.3 %collective-permute-start.14 = (bf16[2,8192]{1,0:T(2,128)(2,1)S(1)}, bf16[2,8192]{1,0:T(2,128)(2,1)S(1)}, u32[]{:S(2)}, u32[]{:S(2)}) collective-permute-start(bf16[2,8192]{1,0:T(2,128)(2,1)S(1)} %collective-permute-done.13), channel_id=1, source_target_pairs={{1,0},{2,1},{3,2},{4,3},{5,4},{6,5},{7,6},{8,7},{9,8},{10,9},{11,1... | collective-permute-start | bytes 98312 | tf_op jit(solution)/shard_map/ppermute | solution.py:24
  81.6 1.2 copy-start.2
  82.8 1.7 copy-start.3
  84.5 1.1 copy-start.16
  85.6 1.3 copy-start.1
  85.6 1.3 copy-start.7
  85.7 1.3 copy-start.22
  88.5 1.3 copy-start.24
  88.5 1.3 copy-start.31
  89.8 0.8 copy-start.14
  90.5 1.6 copy-start.25
  90.5 1.6 copy-start.32
  92.1 2.0 %copy-start.20 = (s32[32]{0:T(128)S(1)}, s32[32]{0:T(128)}, u32[]{:S(2)}) copy-start(s32[32]{0:T(128)} %copy-done.19) | copy-start | bytes 388
  95.6 79.8 %copy-start.9 = (pred[32]{0:T(512)(128)(4,1)S(1)}, pred[32]{0:T(512)(128)(4,1)}, u32[]{:S(2)}) copy-start(pred[32]{0:T(512)(128)(4,1)} %copy-done.8) | copy-start | bytes 100
  95.6 79.8 %copy-start.34 = (f32[32]{0:T(128)S(1)}, f32[32]{0:T(128)}, u32[]{:S(2)}) copy-start(f32[32]{0:T(128)} %compare_convert_fusion) | copy-start | bytes 388
  172.3 4.8 %copy-start.10 = (pred[32]{0:T(512)(128)(4,1)S(1)}, pred[32]{0:T(512)(128)(4,1)}, u32[]{:S(2)}) copy-start(pred[32]{0:T(512)(128)(4,1)} %get-tuple-element.26) | copy-start | bytes 100
  172.3 4.8 %copy-start.35 = (f32[32]{0:T(128)S(1)}, f32[32]{0:T(128)}, u32[]{:S(2)}) copy-start(f32[32]{0:T(128)} %compare_convert_fusion.1) | copy-start | bytes 388
  177.1 1.7 copy-start.5
  177.1 1.7 copy-start.30
  177.1 1.6 copy-start.36
  (4 other events, 2.6 us)
